TPU v7x, 128 devices: a whole 4x4x4 slice. The times are simulated.
128 devices in a mesh: dp: 16 (over y, z), mp: 8 (over x, core).
Axes of the slice: x: 4, y: 4, z: 4, core: 2. Of those that a mesh axis runs over, the one named last changes fastest.
Arguments:
- hidden_in: bfloat16 [4096, 2304], P('dp'), may hold values from -6 to 6
- attn_gain: float32 [2304], replicated, may hold values from 0.25 to 1.75
- w_query: bfloat16 [2304, 2048], P(None, 'mp'), may hold values from -0.25 to 0.25
- w_key: bfloat16 [2304, 2048], P(None, 'mp'), may hold values from -0.125 to 0.125
- w_value: bfloat16 [2304, 2048], P(None, 'mp'), may hold values from -0.125 to 0.125
- w_out: bfloat16 [2048, 2304], P('mp'), may hold values from -0.5 to 0.5
- root_cache: bfloat16 [2, 4096, 2048], P(None, 'dp', 'mp'), may hold values from -400 to 400
- mid_cache: bfloat16 [2, 16, 1024, 2048], P(None, 'dp', None, 'mp'), may hold values from -400 to 400
- leaf_cache: bfloat16 [2, 32, 1024, 2048], P(None, 'dp', None, 'mp'), may hold values from -400 to 400
- mid_len: int32 [16], P('dp'), may hold values from 1 to 1024, 8192 in all
- leaf_len: int32 [32], P('dp'), may hold values from 1 to 1024, 16384 in all
- leaf_of: int32 [128], P('dp'), may hold values from 0 to 31, as said below
- parents: int32 [32], replicated, may hold values from 0 to 15, as said below
- suffix_len: int32 [128], P('dp'), may hold values from 1 to 32, 3072 in all
- ffn_gain: float32 [2304], replicated, may hold values from 0.25 to 1.75
- w_router: float32 [2304, 8], replicated, may hold values from -0.5 to 0.5
- routes: int32 [4096, 2], P('dp'), may hold values from 0 to 7, all different within a row; in each aligned block of 256 rows (0 to 255, 256 to 511, ...) at most 96 rows name the same one
- w_gate: bfloat16 [8, 2304, 5760], P('mp', None, 'dp'), may hold values from -0.125 to 0.125
- w_up: bfloat16 [8, 2304, 5760], P('mp', None, 'dp'), may hold values from -0.125 to 0.125
- w_down: bfloat16 [8, 5760, 2304], P('mp', 'dp'), may hold values from -0.078125 to 0.078125
Outputs:
- layer_out: bfloat16 [4096, 2304], P(('dp', 'mp'))
Inputs may be any that keep to these rules, and one draw needn't show every extreme that they name: `leaf_of`: leaf n belongs to index n // 2 of dp, mid-level node n to index n. The 8 sequences of one index of dp have different mid-level nodes and leaves of one parity, so that no two of them share a mid-level node or a leaf's owner. `parents`: every mid-level node is the parent of exactly one even and one odd leaf. `routes`: in the rows of one index of dp no expert is named by more than 96 rows; some indices of dp reach 96.
All inputs are finite; a program needn't handle non-finite values. No bound on the sum of `mid_len` or of `leaf_len` or of `suffix_len` on one device may be relied on, other than what follows from the above.
Results may differ from a plain program's by a relative error of at most 0.015.
The roundings to bfloat16 on the way count: a program that leaves them out, or rounds other values in their place, can miss the bound.
Values may be sent and summed in bfloat16 or wider, within the bound.
A program may use at most 128 MiB of HBM per device.

v0:
```python
import math
import jax
import jax.numpy as jnp
from jax import lax
from jax.sharding import PartitionSpec as P

HD = 64
TOP = 2
EPS = 1e-05
NEGATIVE = -1e30


def rms_scale(rows, gain):
    rows_wide = rows.astype(jnp.float32)
    mean_square = jnp.mean(rows_wide * rows_wide, axis=-1, keepdims=True)
    return rows_wide * lax.rsqrt(mean_square + EPS) * gain


def level_partial(queries, node_keys, node_values, limits, heads_here, batched):
    senders, row_count, width = queries.shape
    head_dim = width // heads_here
    scale = 1.0 / math.sqrt(head_dim)
    query_heads = queries.reshape(senders, row_count, heads_here, head_dim)
    if batched:
        key_heads = node_keys.reshape(senders, -1, heads_here, head_dim)
        value_heads = node_values.reshape(senders, -1, heads_here, head_dim)
        scores = jnp.einsum(
            "sqhd,skhd->sqhk", query_heads, key_heads, preferred_element_type=jnp.float32
        )
    else:
        key_heads = node_keys.reshape(-1, heads_here, head_dim)
        value_heads = node_values.reshape(-1, heads_here, head_dim)
        scores = jnp.einsum(
            "sqhd,khd->sqhk", query_heads, key_heads, preferred_element_type=jnp.float32
        )
    scores = scores * scale
    slots = jnp.arange(scores.shape[-1], dtype=jnp.int32)
    allowed = slots[None, :] < limits[:, None]
    scores = jnp.where(allowed[:, None, None, :], scores, NEGATIVE)
    peak = jnp.max(scores, axis=-1)
    weights = jnp.exp(scores - peak[..., None])
    total = jnp.sum(weights, axis=-1)
    probs = weights.astype(jnp.bfloat16)
    if batched:
        summed = jnp.einsum(
            "sqhk,skhd->sqhd", probs, value_heads, preferred_element_type=jnp.float32
        )
    else:
        summed = jnp.einsum(
            "sqhk,khd->sqhd", probs, value_heads, preferred_element_type=jnp.float32
        )
    result = (summed / total[..., None]).reshape(senders, row_count, width)
    return (result, peak + jnp.log(total))


def on_device(
    hidden_in,
    attn_gain,
    w_query,
    w_key,
    w_value,
    w_out,
    root_cache,
    mid_cache,
    leaf_cache,
    mid_len,
    leaf_len,
    leaf_of,
    parents,
    suffix_len,
    ffn_gain,
    w_router,
    routes,
    w_gate,
    w_up,
    w_down,
):
    tok_rows, width = hidden_in.shape
    seq_rows = suffix_len.shape[0]
    suffix = tok_rows // seq_rows
    head_dim = HD
    local_width = w_query.shape[1]
    heads_here = local_width // head_dim
    scale = 1.0 / math.sqrt(head_dim)
    owners = lax.axis_size("dp")
    normed = rms_scale(hidden_in, attn_gain).astype(jnp.bfloat16)
    query = jnp.dot(normed, w_query, preferred_element_type=jnp.float32).astype(jnp.bfloat16)
    key = jnp.dot(normed, w_key, preferred_element_type=jnp.float32).astype(jnp.bfloat16)
    value = jnp.dot(normed, w_value, preferred_element_type=jnp.float32).astype(jnp.bfloat16)
    query_heads = query.reshape(tok_rows, heads_here, head_dim)
    piece = lax.all_gather(root_cache, "dp", axis=1, tiled=True)
    running_peak = jnp.full((tok_rows, heads_here), NEGATIVE, jnp.float32)
    piece_keys = piece[0].reshape(-1, heads_here, head_dim)
    piece_values = piece[1].reshape(-1, heads_here, head_dim)
    scores = (
        jnp.einsum("qhd,khd->qhk", query_heads, piece_keys, preferred_element_type=jnp.float32)
        * scale
    )
    new_peak = jnp.maximum(running_peak, jnp.max(scores, axis=-1))
    weights = jnp.exp(scores - new_peak[..., None])
    new_total = jnp.sum(weights, axis=-1)
    added = jnp.einsum(
        "qhk,khd->qhd",
        weights.astype(jnp.bfloat16),
        piece_values,
        preferred_element_type=jnp.float32,
    )
    root_out = added / new_total[..., None]
    root_lse = new_peak + jnp.log(new_total)
    query_seq = query.reshape(seq_rows, suffix, heads_here, head_dim)
    key_seq = key.reshape(seq_rows, suffix, heads_here, head_dim)
    value_seq = value.reshape(seq_rows, suffix, heads_here, head_dim)
    slots = jnp.arange(suffix, dtype=jnp.int32)
    self_ok = (slots[None, None, :] <= slots[None, :, None]) & (
        slots[None, None, :] < suffix_len[:, None, None]
    )
    self_scores = (
        jnp.einsum("sqhd,skhd->sqhk", query_seq, key_seq, preferred_element_type=jnp.float32)
        * scale
    )
    self_scores = jnp.where(self_ok[:, :, None, :], self_scores, NEGATIVE)
    self_peak = jnp.max(self_scores, axis=-1)
    self_weights = jnp.exp(self_scores - self_peak[..., None])
    self_total = jnp.sum(self_weights, axis=-1)
    self_sum = jnp.einsum(
        "sqhk,skhd->sqhd",
        self_weights.astype(jnp.bfloat16),
        value_seq,
        preferred_element_type=jnp.float32,
    )
    self_out = (self_sum / self_total[..., None]).reshape(tok_rows, heads_here, head_dim)
    self_lse = (self_peak + jnp.log(self_total)).reshape(tok_rows, heads_here)
    mid_of = parents[leaf_of]
    leaf_owner = leaf_of // 2
    targets = jnp.arange(owners, dtype=jnp.int32)
    pick_mid = (mid_of[None, :] == targets[:, None]).astype(jnp.bfloat16)
    pick_leaf = (leaf_owner[None, :] == targets[:, None]).astype(jnp.bfloat16)
    flat_query = query.reshape(seq_rows, suffix * local_width)
    sent_mid = jnp.dot(pick_mid, flat_query, preferred_element_type=jnp.float32).astype(
        jnp.bfloat16
    )
    sent_leaf = jnp.dot(pick_leaf, flat_query, preferred_element_type=jnp.float32).astype(
        jnp.bfloat16
    )
    sent = jnp.stack([sent_mid, sent_leaf], axis=1).reshape(owners, 2, suffix, local_width)
    sent_queries = lax.all_to_all(sent, "dp", split_axis=0, concat_axis=0, tiled=True)
    leaf_every = lax.all_gather(leaf_of, "dp", axis=0, tiled=True).reshape(owners, seq_rows)
    me_dp = lax.axis_index("dp")
    second = jnp.any((leaf_every // 2 == me_dp) & (leaf_every % 2 == 1), axis=1)
    senders = sent_queries.shape[0]
    mid_limit = jnp.broadcast_to(mid_len[0], (senders,))
    mid_result, mid_logsum = level_partial(
        sent_queries[:, 0], mid_cache[0, 0], mid_cache[1, 0], mid_limit, heads_here, False
    )
    leaf_keys = jnp.where(second[:, None, None], leaf_cache[0, 1][None], leaf_cache[0, 0][None])
    leaf_values = jnp.where(second[:, None, None], leaf_cache[1, 1][None], leaf_cache[1, 0][None])
    leaf_limit = jnp.where(second, leaf_len[1], leaf_len[0])
    leaf_result, leaf_logsum = level_partial(
        sent_queries[:, 1], leaf_keys, leaf_values, leaf_limit, heads_here, True
    )
    owner_out = jnp.stack([mid_result, leaf_result], axis=1)
    owner_lse = jnp.stack([mid_logsum, leaf_logsum], axis=1)
    owner_all = jnp.concatenate([owner_out, owner_lse], axis=-1)
    back_all = lax.all_to_all(owner_all, "dp", split_axis=0, concat_axis=0, tiled=True)
    back_out = back_all[..., :local_width]
    back_lse = back_all[..., local_width:]
    mid_out = back_out[mid_of, 0].reshape(tok_rows, heads_here, head_dim)
    mid_lse = back_lse[mid_of, 0].reshape(tok_rows, heads_here)
    leaf_out = back_out[leaf_owner, 1].reshape(tok_rows, heads_here, head_dim)
    leaf_lse = back_lse[leaf_owner, 1].reshape(tok_rows, heads_here)
    stacked_lse = jnp.stack([root_lse, mid_lse, leaf_lse, self_lse])
    stacked_out = jnp.stack([root_out, mid_out, leaf_out, self_out])
    overall = jnp.max(stacked_lse, axis=0)
    shares = jnp.exp(stacked_lse - overall)
    combined = jnp.sum(shares[..., None] * stacked_out, axis=0) / jnp.sum(shares, axis=0)[..., None]
    attended = combined.reshape(tok_rows, local_width).astype(jnp.bfloat16)
    projected = jnp.dot(attended, w_out, preferred_element_type=jnp.float32)
    rows_here = tok_rows // lax.axis_size("mp")
    first = lax.axis_index("mp") * rows_here
    attn_rows = lax.psum_scatter(projected, "mp", scatter_dimension=0, tiled=True)
    resid = lax.dynamic_slice_in_dim(hidden_in, first, rows_here, 0).astype(jnp.float32) + attn_rows
    ffn_rows = rms_scale(resid, ffn_gain).astype(jnp.bfloat16)
    ffn_in = lax.all_gather(ffn_rows, "mp", axis=0, tiled=True)
    logits = jnp.dot(ffn_in.astype(jnp.float32), w_router, precision=lax.Precision.HIGHEST)
    chosen = jnp.take_along_axis(logits, routes, axis=1)
    squashed = jax.nn.sigmoid(chosen)
    gates = squashed / jnp.sum(squashed, axis=1, keepdims=True)
    expert = lax.axis_index("mp")
    hit_each = routes == expert
    hit = jnp.any(hit_each, axis=1)
    gate_here = jnp.sum(jnp.where(hit_each, gates, 0.0), axis=1)
    order = jnp.cumsum(hit.astype(jnp.int32)) - 1
    capacity = 3 * TOP * tok_rows // (2 * lax.axis_size("mp"))
    slot_ids = jnp.arange(capacity, dtype=jnp.int32)
    pick_slot = (order[None, :] == slot_ids[:, None]) & hit[None, :]
    dispatch = jnp.dot(
        pick_slot.astype(jnp.bfloat16), ffn_in, preferred_element_type=jnp.float32
    ).astype(jnp.bfloat16)
    slot_gate = jnp.dot(pick_slot.astype(jnp.float32), gate_here, precision=lax.Precision.HIGHEST)
    gate_weight = w_gate[0]
    up_weight = w_up[0]
    down_weight = w_down[0]
    piece = lax.all_gather(dispatch, "dp", axis=0, tiled=True)
    gate_part = jnp.dot(piece, gate_weight, preferred_element_type=jnp.float32)
    up_part = jnp.dot(piece, up_weight, preferred_element_type=jnp.float32)
    partial_out = jnp.dot(
        (jax.nn.silu(gate_part) * up_part).astype(jnp.bfloat16),
        down_weight,
        preferred_element_type=jnp.float32,
    )
    expert_out = lax.psum_scatter(
        partial_out.astype(jnp.bfloat16), "dp", scatter_dimension=0, tiled=True
    )
    weighted = expert_out.astype(jnp.float32) * slot_gate[:, None]
    spread = jnp.dot(pick_slot.astype(jnp.float32).T, weighted, precision=lax.Precision.HIGHEST)
    mixed = lax.psum_scatter(
        spread.astype(jnp.bfloat16), "mp", scatter_dimension=0, tiled=True
    ).astype(jnp.float32)
    row_ids = first + jnp.arange(rows_here, dtype=jnp.int32)
    valid = row_ids % suffix < suffix_len[row_ids // suffix]
    return jnp.where(valid[:, None], resid + mixed, 0.0).astype(jnp.bfloat16)


def solution(mesh):
    return jax.shard_map(
        on_device,
        mesh=mesh,
        in_specs=(
            P("dp", None),
            P(),
            P(None, "mp"),
            P(None, "mp"),
            P(None, "mp"),
            P("mp", None),
            P(None, "dp", "mp"),
            P(None, "dp", None, "mp"),
            P(None, "dp", None, "mp"),
            P("dp"),
            P("dp"),
            P("dp"),
            P(),
            P("dp"),
            P(),
            P(),
            P("dp", None),
            P("mp", None, "dp"),
            P("mp", None, "dp"),
            P("mp", "dp", None),
        ),
        out_specs=P(("dp", "mp"), None),
        check_vma=False,
    )
```

profile of v0, /device:TPU:0, one launch (start us, length us, event | category | flops | bytes accessed | tf_op | source)
XLA Modules:
  0.0 436.8 jit_solution(13475134126374077228)
XLA Ops:
  7.3 1.6 fusion.30
  9.6 2.4 convolution_convert_fusion.7
  14.9 8.2 %all-to-all-start = ((bf16[16,2,32,256]{3,2,1,0:T(8,128)(2,1)}), bf16[16,2,32,256]{3,2,1,0:T(8,128)(2,1)}, u32[]{:S(2)}, u32[]{:S(2)}) async-start(bf16[16,2,32,256]{3,2,1,0:T(8,128)(2,1)} %pad_maximum_fusion.1), calls=%async_computation | async-start | bytes 1048576 | tf_op jit(solution)/shard_map/all_to_all | solution.py:146
  24.6 17.4 %all-reduce.2 = s32[128]{0:T(128)S(1)} all-reduce(s32[128]{0:T(128)S(1)} %dynamic-update-slice), channel_id=1, replica_groups=mesh['dp'=16,'mp'=8] {'dp'}, use_global_device_ids=true, to_apply=%add.2 | all-reduce | flops 128 | bytes 1024
  42.9 1.3 broadcast_select_fusion
  44.9 2.2 fusion.126
  47.2 2.5 convolution_convert_fusion.6
  49.7 1.2 fusion.125
  53.8 2.1 copy.294
  56.0 2.1 copy.296
  60.2 2.0 fusion.129
  64.6 4.3 bitcast_reduce_fusion.1
  68.9 2.6 fusion.15
  71.6 2.7 fusion.58
  75.1 1.4 stack_reshape.23
  76.5 2.4 bitcast_reduce_fusion.2
  78.9 2.0 fusion.13
  80.9 1.8 fusion.63
  83.5 1.4 stack_reshape.22
  85.2 2.4 pad_maximum_fusion
  87.6 5.1 %all-to-all-start.1 = ((f32[16,2,32,260]{3,2,1,0:T(8,128)}), f32[16,2,32,260]{3,2,1,0:T(8,128)S(1)}, u32[]{:S(2)}, u32[]{:S(2)}) async-start(f32[16,2,32,260]{3,2,1,0:T(8,128)} %pad_maximum_fusion), calls=%async_computation.1 | async-start | bytes 3145728 | tf_op jit(solution)/shard_map/all_to_all | solution.py:164
  92.9 1.2 fusion.74
  94.3 2.8 convolution_convert_fusion.5
  98.2 1.4 fusion.45
  100.4 1.9 copy.288
  102.3 10.9 %all-to-all-done.1 = f32[16,2,32,260]{3,2,1,0:T(8,128)S(1)} async-done(((f32[16,2,32,260]{3,2,1,0:T(8,128)}), f32[16,2,32,260]{3,2,1,0:T(8,128)S(1)}, u32[]{:S(2)}, u32[]{:S(2)}) %all-to-all-start.1) | async-done | bytes 1064992 | tf_op jit(solution)/shard_map/all_to_all | solution.py:164
  114.1 1.3 copy.298
  118.0 1.8 gather_fusion.4
  119.8 1.8 gather_fusion.5
  122.5 4.5 %fusion.124 = (bf16[1,4096,256]{2,1,0:T(8,128)(2,1)}, bf16[1,4096,256]{2,1,0:T(8,128)(2,1)}) fusion(bf16[2,4096,256]{2,1,0:T(8,128)(2,1)} %all-gather.4.cloned.1.call-done), kind=kLoop, calls=%fused_computation.185 | loop fusion | bytes 8388608 | tf_op jit(solution)/shard_map/slice | solution.py:93
  127.0 4.1 copy.253
  131.1 4.2 copy.282
  135.2 9.7 %bitcast_reduce_fusion = (f32[256,4]{0,1:T(4,128)S(1)}, f32[4,256,4096]{2,1,0:T(8,128)}) fusion(bf16[256,4,64]{0,2,1:T(8,128)(2,1)S(1)} %bitcast.190, bf16[4096,4,64]{0,2,1:T(8,128)(2,1)} %bitcast.174), kind=kOutput, calls=%fused_computation.8 | convolution fusion | flops 545258496 | bytes 19009536 | tf_op jit(solution)/shard_map/qhd,khd->qhk/dot_general | solution.py:96
  144.9 8.6 %fusion.2 = f32[256,4]{0,1:T(4,128)S(1)} fusion(f32[4,256,4096]{2,1,0:T(8,128)} %get-tuple-element.33, f32[256,4]{0,1:T(4,128)S(1)} %broadcast_maximum_fusion), kind=kLoop, calls=%fused_computation.11 | loop fusion | flops 12581888 | bytes 16785408 | tf_op jit(solution)/shard_map/reduce_sum | solution.py:101
  153.6 8.1 %fusion.54 = f32[1,256,4,64]{1,3,2,0:T(8,128)S(1)} fusion(bf16[4096,4,64]{0,2,1:T(8,128)(2,1)} %bitcast.176, f32[4,256,4096]{2,1,0:T(8,128)} %get-tuple-element.33, f32[256,4]{0,1:T(4,128)S(1)} %broadcast_maximum_fusion, f32[256,4]{0,1:T(4,128)S(1)} %fusion.2), kind=kOutput, calls=%fused_computation.71 | convolution fusion | flops 549519360 | bytes 19144704 | tf_op jit(solution)/shard_map/qhk,khd->qhd/dot_general | solution.py:102
  163.0 1.9 fusion.130
  165.0 31.7 %reduce-scatter.4.cloned.1.call-done = f32[32,2304]{1,0:T(8,128)} async-done(((f32[256,2304]{1,0:T(8,128)}), f32[32,2304]{1,0:T(8,128)}) %reduce-scatter.4.cloned.1.call-update) | async-done | bytes 294928 | tf_op jit(solution)/shard_map/reduce_scatter | solution.py:180
  197.8 1.8 multiply_convert_fusion
  200.3 21.9 %all-gather.6.cloned.1.call-done = bf16[256,2304]{1,0:T(8,128)(2,1)} async-done(((bf16[32,2304]{1,0:T(8,128)(2,1)}), bf16[256,2304]{1,0:T(8,128)(2,1)}) %all-gather.6.cloned.1.call-update) | async-done | bytes 1179664 | tf_op jit(solution)/shard_map/all_gather | solution.py:183
  222.2 2.4 convolution_convert_fusion.4
  224.9 65.0 %all-gather.8.cloned.1.call-done = bf16[1536,2304]{1,0:T(8,128)(2,1)} async-done(((bf16[96,2304]{1,0:T(8,128)(2,1)}), bf16[1536,2304]{1,0:T(8,128)(2,1)}) %all-gather.8.cloned.1.call-update) | async-done | bytes 7077904 | tf_op jit(solution)/shard_map/all_gather | solution.py:203
  289.9 7.6 %fusion.35 = f32[1536,360]{0,1:T(8,128)} fusion(bf16[1536,2304]{1,0:T(8,128)(2,1)} %all-gather.8.cloned.1.call-done, bf16[1,2304,360]{1,2,0:T(8,128)(2,1)} %param.37), kind=kOutput, calls=%fused_computation.55 | convolution fusion | flops 2548039680 | bytes 10948608 | tf_op jit(solution)/shard_map/dot_general | solution.py:204
  297.5 13.1 %convolution_convert_fusion = bf16[1536,2304]{1,0:T(8,128)(2,1)} fusion(bf16[1,360,2304]{2,1,0:T(8,128)(2,1)S(1)} %copy-done, bf16[1536,2304]{1,0:T(8,128)(2,1)} %all-gather.8.cloned.1.call-done, f32[1536,360]{0,1:T(8,128)} %fusion.35, bf16[1,2304,360]{1,2,0:T(8,128)(2,1)} %param.38), kind=kOutput, calls=%fused_computation.12 | convolution fusion | flops 5102936064 | bytes 19685376 | tf_op jit(solution)/shard_map/dot_general | solution.py:206
  312.9 3.6 gather_fusion.6
  316.9 76.4 %reduce-scatter.6.cloned.1.call-done = bf16[96,2304]{1,0:T(8,128)(2,1)} async-done(((bf16[1536,2304]{1,0:T(8,128)(2,1)}), bf16[96,2304]{1,0:T(8,128)(2,1)}) %reduce-scatter.6.cloned.1.call-update) | async-done | bytes 442384 | tf_op jit(solution)/shard_map/reduce_scatter | solution.py:211
  393.3 3.2 convolution_convert_fusion.3
  397.3 30.7 %reduce-scatter.8.cloned.1.call-done = bf16[32,2304]{1,0:T(8,128)(2,1)} async-done(((bf16[256,2304]{1,0:T(8,128)(2,1)}), bf16[32,2304]{1,0:T(8,128)(2,1)}) %reduce-scatter.8.cloned.1.call-update) | async-done | bytes 147472 | tf_op jit(solution)/shard_map/reduce_scatter | solution.py:216
  428.0 1.7 select_convert_fusion
  (151 shorter events, 28.8 us)
Async XLA Ops:
  6.5 290.9 %copy-start = (bf16[1,360,2304]{2,1,0:T(8,128)(2,1)S(1)}, bf16[1,360,2304]{2,1,0:T(8,128)(2,1)}, u32[]{:S(2)}) copy-start(bf16[1,360,2304]{2,1,0:T(8,128)(2,1)} %param.39) | copy-start | bytes 4976644
  6.5 116.0 %all-gather.4.cloned.1.call-start = ((), (), s32[]{:S(2)}) async-start(), calls=%async_computation.5 | async-start | bytes 4456448 | tf_op jit(solution)/shard_map/all_gather | solution.py:91
  9.5 3.5 copy-start.2
  11.9 0.7 copy-start.16
  12.7 10.4 %copy-start.26 = (u32[128]{0:T(128)S(1)}, u32[128]{0:T(128)}, u32[]{:S(2)}) copy-start(u32[128]{0:T(128)} %constant.214) | copy-start | bytes 1540
  12.7 11.7 %copy-start.24 = (s32[8]{0:T(128)S(1)}, s32[8]{0:T(128)}, u32[]{:S(2)}) copy-start(s32[8]{0:T(128)} %param.31) | copy-start | bytes 100
  12.7 29.3 %copy-start.3 = (s32[8]{0:T(128)S(1)}, s32[8]{0:T(128)}, u32[]{:S(2)}) copy-start(s32[8]{0:T(128)} %param.33) | copy-start | bytes 100
  12.7 29.3 %copy-start.23 = (s32[2]{0:T(128)S(1)}, s32[2]{0:T(128)}, u32[]{:S(2)}) copy-start(s32[2]{0:T(128)} %param.30) | copy-start | bytes 28
  14.0 33.2 %copy-start.6 = (bf16[256,2304]{1,0:T(8,128)(2,1)S(1)}, bf16[256,2304]{1,0:T(8,128)(2,1)}, u32[]{:S(2)}) copy-start(bf16[256,2304]{1,0:T(8,128)(2,1)} %param.20) | copy-start | bytes 3538948
  14.9 47.3 %all-to-all-start = ((bf16[16,2,32,256]{3,2,1,0:T(8,128)(2,1)}), bf16[16,2,32,256]{3,2,1,0:T(8,128)(2,1)}, u32[]{:S(2)}, u32[]{:S(2)}) async-start(bf16[16,2,32,256]{3,2,1,0:T(8,128)(2,1)} %pad_maximum_fusion.1), calls=%async_computation | async-start | bytes 1048576 | tf_op jit(solution)/shard_map/all_to_all | solution.py:146
  44.9 4.7 %copy-start.7 = (bf16[2,2,1024,256]{3,2,1,0:T(8,128)(2,1)S(1)}, bf16[2,2,1024,256]{3,2,1,0:T(8,128)(2,1)}, u32[]{:S(2)}) copy-start(bf16[2,2,1024,256]{3,2,1,0:T(8,128)(2,1)} %param.28) | copy-start | bytes 6291460
  49.7 2.1 copy-start.19
  49.7 3.9 copy-start.9
  53.8 4.2 copy-start.10
  53.8 6.4 %copy-start.18 = (bf16[8,32,4,64]{3,2,1,0:T(4,128)(2,1)S(1)}, bf16[8,32,4,64]{3,2,1,0:T(4,128)(2,1)}, u32[]{:S(2)}) copy-start(bf16[8,32,4,64]{3,2,1,0:T(4,128)(2,1)} %reshape.404) | copy-start | bytes 393220
  68.9 2.7 copy-start.14
  68.9 2.7 copy-start.15
  78.9 2.0 copy-start.13
  82.8 2.5 copy-start.8
  87.6 6.6 %copy-start.25 = (f32[2304]{0:T(1024)S(1)}, f32[2304]{0:T(1024)}, u32[]{:S(2)}) copy-start(f32[2304]{0:T(1024)} %param.21) | copy-start | bytes 27652
  87.6 25.6 %all-to-all-start.1 = ((f32[16,2,32,260]{3,2,1,0:T(8,128)}), f32[16,2,32,260]{3,2,1,0:T(8,128)S(1)}, u32[]{:S(2)}, u32[]{:S(2)}) async-start(f32[16,2,32,260]{3,2,1,0:T(8,128)} %pad_maximum_fusion), calls=%async_computation.1 | async-start | bytes 3145728 | tf_op jit(solution)/shard_map/all_to_all | solution.py:164
  92.7 104.0 %reduce-scatter.4.cloned.1.call-start = ((), (), s32[]{:S(2)}) async-start(), calls=%async_computation.6 | async-start | bytes 2654208 | tf_op jit(solution)/shard_map/reduce_scatter | solution.py:180
  131.1 4.2 copy-start.17
  153.6 8.2 %copy-start.12 = (f32[1,256,4,64]{1,3,2,0:T(8,128)S(1)}, f32[1,256,4,64]{1,3,2,0:T(8,128)}, u32[]{:S(2)}) copy-start(f32[1,256,4,64]{1,3,2,0:T(8,128)} %copy.288) | copy-start | bytes 786436
  161.7 1.3 copy-start.11
  163.0 34.8 %copy-start.22 = (f32[2304]{0:T(1024)S(1)}, f32[2304]{0:T(1024)}, u32[]{:S(2)}) copy-start(f32[2304]{0:T(1024)} %param.34) | copy-start | bytes 27652
  164.9 34.8 %copy-start.21 = (s32[256,2]{0,1:T(2,128)S(1)}, s32[256,2]{0,1:T(2,128)}, u32[]{:S(2)}) copy-start(s32[256,2]{0,1:T(2,128)} %param.36) | copy-start | bytes 6148
  164.9 57.3 %all-gather.6.cloned.1.call-start = ((), (), s32[]{:S(2)}) async-start(), calls=%async_computation.7 | async-start | bytes 1327104 | tf_op jit(solution)/shard_map/all_gather | solution.py:183
  199.6 90.3 %all-gather.8.cloned.1.call-start = ((), (), s32[]{:S(2)}) async-start(), calls=%async_computation.8 | async-start | bytes 7520256 | tf_op jit(solution)/shard_map/all_gather | solution.py:203
  224.6 168.7 %reduce-scatter.6.cloned.1.call-start = ((), (), s32[]{:S(2)}) async-start(), calls=%async_computation.9 | async-start | bytes 7520256 | tf_op jit(solution)/shard_map/reduce_scatter | solution.py:211
  310.6 1.3 copy-start.4
  310.6 1.3 copy-start.20
  310.6 117.3 %reduce-scatter.8.cloned.1.call-start = ((), (), s32[]{:S(2)}) async-start(), calls=%async_computation.10 | async-start | bytes 1327104 | tf_op jit(solution)/shard_map/reduce_scatter | solution.py:216
  312.9 116.8 %copy-start.1 = (bf16[1,360,2304]{2,1,0:T(8,128)(2,1)S(1)}, bf16[1,360,2304]{2,1,0:T(8,128)(2,1)}, u32[]{:S(2)}) copy-start(bf16[1,360,2304]{2,1,0:T(8,128)(2,1)} %param.39) | copy-start | bytes 4976644
  316.4 111.5 %copy-start.5 = (f32[32,2304]{1,0:T(8,128)S(1)}, f32[32,2304]{1,0:T(8,128)}, u32[]{:S(2)}) copy-start(f32[32,2304]{1,0:T(8,128)} %reduce-scatter.4.cloned.1.call-done) | copy-start | bytes 884740
Sparse Core Ops, SparseCore 0:
  9.6 57.6 all-gather.3
  165.0 31.5 reduce-scatter.3
  199.7 22.4 all-gather.5
  224.7 65.1 all-gather.7
  310.8 82.4 reduce-scatter.5
  396.6 31.2 reduce-scatter.7
where the time goes:
time: 444 us; the launch traced here: 437 us
  waiting for transfers between devices  237 us (53%)
  matrix products  69.9 us (16%)
  local copies, waits for them, and re-layouts  55.5 us (12%)
  other arithmetic  27.1 us (6%)
  blocking collectives  17.4 us (4%)
  between operations  15.6 us (4%)
  starting transfers between devices  13.8 us (3%)
    reduce_scatter x1, waiting for transfers between devices, on_device(): lax.psum_scatter(partial_out.astype(jnp.bfloat16), 'dp', scatter_dimensio...  76.4 us
    all_gather x1, waiting for transfers between devices, on_device(): piece = lax.all_gather(dispatch, 'dp', axis=0, tiled=True)  65 us
    reduce_scatter x1, waiting for transfers between devices, on_device(): lax.psum_scatter(projected, 'mp', scatter_dimension=0, tiled=True)  31.7 us
    reduce_scatter x1, waiting for transfers between devices, on_device(): lax.psum_scatter(spread.astype(jnp.bfloat16), 'mp', scatter_dimension=0,...  30.7 us
    all_gather x1, waiting for transfers between devices, on_device(): ffn_in = lax.all_gather(ffn_rows, 'mp', axis=0, tiled=True)  21.9 us
    unnamed x1, blocking collectives  17.4 us
    dot_general x1, matrix products, on_device(): jnp.dot((jax.nn.silu(gate_part) * up_part).astype(jnp.bfloat16), down_wei...  13.1 us
    unnamed x64, local copies, waits for them, and re-layouts  11.2 us
  transfers between devices with their start and end apart: 8, of which 6 were waited for; matrix products, arithmetic and copies ran while one was open for 18% of the time, Pallas kernels for 0%

commit v1 on v0

--- a/solution.py
+++ b/solution.py
@@ -200,7 +200,9 @@
     gate_weight = w_gate[0]
     up_weight = w_up[0]
     down_weight = w_down[0]
-    piece = lax.all_gather(dispatch, "dp", axis=0, tiled=True)
+    piece = jnp.concatenate(
+        lax.all_to_all(jnp.stack([dispatch] * lax.axis_size("dp")), "dp", 0, 0), axis=0
+    )
     gate_part = jnp.dot(piece, gate_weight, preferred_element_type=jnp.float32)
     up_part = jnp.dot(piece, up_weight, preferred_element_type=jnp.float32)
     partial_out = jnp.dot(

time: 444 us -> 464 us (1.045)
  blocking collectives: 17.4 us -> 106 us
  waiting for transfers between devices: 237 us -> 169 us
    all_to_all x0 -> x1, blocking collectives: none -> 88.9 us  [on_device(): lax.all_to_all(jnp.stack([dispatch] * lax.axis_size('dp')), 'dp', 0, 0)]
    all_gather x1 -> x0, waiting for transfers between devices: 65 us -> none  [on_device(): piece = lax.all_gather(dispatch, 'dp', axis=0, tiled=True)]
    unnamed x64 -> x66, local copies, waits for them, and re-layouts: 11.2 us -> 14.1 us
  transfers between devices with their start and end apart: 8 -> 7, of which waited for: 6 -> 5; matrix products, arithmetic and copies ran while one was open for 18% -> 17% of each run, Pallas kernels for 0% -> 0%
where the time goes in v1:
time: 464 us; the launch traced here: 456 us
  waiting for transfers between devices  169 us (36%)
  blocking collectives  106 us (23%)
  matrix products  65.7 us (14%)
  local copies, waits for them, and re-layouts  59.1 us (13%)
  other arithmetic  27.1 us (6%)
  between operations  15.3 us (3%)
  starting transfers between devices  13.8 us (3%)
    all_to_all x1, blocking collectives, on_device(): lax.all_to_all(jnp.stack([dispatch] * lax.axis_size('dp')), 'dp', 0, 0)  88.9 us
    reduce_scatter x1, waiting for transfers between devices, on_device(): lax.psum_scatter(partial_out.astype(jnp.bfloat16), 'dp', scatter_dimensio...  73.2 us
    reduce_scatter x1, waiting for transfers between devices, on_device(): lax.psum_scatter(projected, 'mp', scatter_dimension=0, tiled=True)  31.7 us
    reduce_scatter x1, waiting for transfers between devices, on_device(): lax.psum_scatter(spread.astype(jnp.bfloat16), 'mp', scatter_dimension=0,...  30.7 us
    all_gather x1, waiting for transfers between devices, on_device(): ffn_in = lax.all_gather(ffn_rows, 'mp', axis=0, tiled=True)  21.8 us
    unnamed x1, blocking collectives  17.4 us
    unnamed x66, local copies, waits for them, and re-layouts  14.1 us
    dot_general x1, matrix products, on_device(): jnp.dot((jax.nn.silu(gate_part) * up_part).astype(jnp.bfloat16), down_wei...  13.1 us
  transfers between devices with their start and end apart: 7, of which 5 were waited for; matrix products, arithmetic and copies ran while one was open for 17% of the time, Pallas kernels for 0%

profile of v1, /device:TPU:0, one launch (start us, length us, event | category | flops | bytes accessed | tf_op | source)
XLA Modules:
  0.0 456.4 jit_solution(16208910190513061712)
XLA Ops:
  7.3 1.6 fusion.30
  9.6 2.4 convolution_convert_fusion.7
  14.9 8.2 %all-to-all-start = ((bf16[16,2,32,256]{3,2,1,0:T(8,128)(2,1)}), bf16[16,2,32,256]{3,2,1,0:T(8,128)(2,1)}, u32[]{:S(2)}, u32[]{:S(2)}) async-start(bf16[16,2,32,256]{3,2,1,0:T(8,128)(2,1)} %pad_maximum_fusion.1), calls=%async_computation | async-start | bytes 1048576 | tf_op jit(solution)/shard_map/all_to_all | solution.py:146
  24.6 17.4 %all-reduce.2 = s32[128]{0:T(128)S(1)} all-reduce(s32[128]{0:T(128)S(1)} %dynamic-update-slice), channel_id=1, replica_groups=mesh['dp'=16,'mp'=8] {'dp'}, use_global_device_ids=true, to_apply=%add.2 | all-reduce | flops 128 | bytes 1024
  42.9 1.3 broadcast_select_fusion
  44.9 2.2 fusion.126
  47.2 2.5 convolution_convert_fusion.6
  53.8 2.1 copy.294
  56.0 2.1 copy.296
  60.2 2.0 fusion.129
  64.6 4.3 bitcast_reduce_fusion.1
  68.9 2.6 fusion.15
  71.6 2.7 fusion.58
  75.1 1.4 stack_reshape.23
  76.5 2.4 bitcast_reduce_fusion.2
  78.9 2.0 fusion.13
  80.9 1.8 fusion.63
  83.5 1.4 stack_reshape.22
  85.2 2.4 pad_maximum_fusion
  87.6 5.1 %all-to-all-start.1 = ((f32[16,2,32,260]{3,2,1,0:T(8,128)}), f32[16,2,32,260]{3,2,1,0:T(8,128)S(1)}, u32[]{:S(2)}, u32[]{:S(2)}) async-start(f32[16,2,32,260]{3,2,1,0:T(8,128)} %pad_maximum_fusion), calls=%async_computation.1 | async-start | bytes 3145728 | tf_op jit(solution)/shard_map/all_to_all | solution.py:164
  92.9 1.2 fusion.74
  94.3 2.8 convolution_convert_fusion.5
  98.2 1.4 fusion.45
  100.4 1.9 copy.288
  102.3 10.9 %all-to-all-done.1 = f32[16,2,32,260]{3,2,1,0:T(8,128)S(1)} async-done(((f32[16,2,32,260]{3,2,1,0:T(8,128)}), f32[16,2,32,260]{3,2,1,0:T(8,128)S(1)}, u32[]{:S(2)}, u32[]{:S(2)}) %all-to-all-start.1) | async-done | bytes 1064992 | tf_op jit(solution)/shard_map/all_to_all | solution.py:164
  114.1 1.3 copy.298
  118.0 1.8 gather_fusion.4
  119.8 1.8 gather_fusion.5
  122.5 4.5 fusion.124
  127.0 4.1 copy.253
  131.1 4.2 copy.282
  135.2 9.7 %bitcast_reduce_fusion = (f32[256,4]{0,1:T(4,128)S(1)}, f32[4,256,4096]{2,1,0:T(8,128)}) fusion(bf16[256,4,64]{0,2,1:T(8,128)(2,1)S(1)} %bitcast.193, bf16[4096,4,64]{0,2,1:T(8,128)(2,1)} %bitcast.175), kind=kOutput, calls=%fused_computation.8 | convolution fusion | flops 545258496 | bytes 19009536 | tf_op jit(solution)/shard_map/qhd,khd->qhk/dot_general | solution.py:96
  144.9 8.6 %fusion.2 = f32[256,4]{0,1:T(4,128)S(1)} fusion(f32[4,256,4096]{2,1,0:T(8,128)} %get-tuple-element.33, f32[256,4]{0,1:T(4,128)S(1)} %broadcast_maximum_fusion), kind=kLoop, calls=%fused_computation.11 | loop fusion | flops 12581888 | bytes 16785408 | tf_op jit(solution)/shard_map/reduce_sum | solution.py:101
  153.6 8.1 %fusion.54 = f32[1,256,4,64]{1,3,2,0:T(8,128)S(1)} fusion(bf16[4096,4,64]{0,2,1:T(8,128)(2,1)} %bitcast.179, f32[4,256,4096]{2,1,0:T(8,128)} %get-tuple-element.33, f32[256,4]{0,1:T(4,128)S(1)} %broadcast_maximum_fusion, f32[256,4]{0,1:T(4,128)S(1)} %fusion.2), kind=kOutput, calls=%fused_computation.71 | convolution fusion | flops 549519360 | bytes 19144704 | tf_op jit(solution)/shard_map/qhk,khd->qhd/dot_general | solution.py:102
  163.0 1.9 fusion.130
  165.0 31.7 %reduce-scatter.4.cloned.1.call-done = f32[32,2304]{1,0:T(8,128)} async-done(((f32[256,2304]{1,0:T(8,128)}), f32[32,2304]{1,0:T(8,128)}) %reduce-scatter.4.cloned.1.call-update) | async-done | bytes 294928 | tf_op jit(solution)/shard_map/reduce_scatter | solution.py:180
  197.8 1.8 multiply_convert_fusion
  200.5 21.8 %all-gather.5.cloned.1.call-done = bf16[256,2304]{1,0:T(8,128)(2,1)} async-done(((bf16[32,2304]{1,0:T(8,128)(2,1)}), bf16[256,2304]{1,0:T(8,128)(2,1)}) %all-gather.5.cloned.1.call-update) | async-done | bytes 1179664 | tf_op jit(solution)/shard_map/all_gather | solution.py:183
  222.3 1.6 convolution_convert_fusion.4
  224.6 88.9 %all_to_all.15 = bf16[16,96,2304]{2,1,0:T(8,128)(2,1)S(1)} all-to-all(bf16[16,96,2304]{2,1,0:T(8,128)(2,1)S(1)} %stack.60), channel_id=1, replica_groups=mesh['dp'=16,'mp'=8] {'dp'}, dimensions={0} | all-to-all | bytes 14155776 | tf_op jit(solution)/shard_map/all_to_all | solution.py:204
  313.5 2.9 copy-done.3
  316.4 4.1 fusion.35
  320.5 13.1 %convolution_convert_fusion = bf16[1536,2304]{1,0:T(8,128)(2,1)} fusion(bf16[1,360,2304]{2,1,0:T(8,128)(2,1)S(1)} %copy-done, bf16[1536,2304]{1,0:T(8,128)(2,1)} %bitcast.177, f32[1536,360]{0,1:T(8,128)} %fusion.35, bf16[1,2304,360]{1,2,0:T(8,128)(2,1)} %param.38), kind=kOutput, calls=%fused_computation.12 | convolution fusion | flops 5102936064 | bytes 19685376 | tf_op jit(solution)/shard_map/dot_general | solution.py:208
  335.9 3.6 gather_fusion.6
  339.9 73.2 %reduce-scatter.6.cloned.1.call-done = bf16[96,2304]{1,0:T(8,128)(2,1)} async-done(((bf16[1536,2304]{1,0:T(8,128)(2,1)}), bf16[96,2304]{1,0:T(8,128)(2,1)}) %reduce-scatter.6.cloned.1.call-update) | async-done | bytes 442384 | tf_op jit(solution)/shard_map/reduce_scatter | solution.py:213
  413.2 3.2 convolution_convert_fusion.3
  417.2 30.7 %reduce-scatter.8.cloned.1.call-done = bf16[32,2304]{1,0:T(8,128)(2,1)} async-done(((bf16[256,2304]{1,0:T(8,128)(2,1)}), bf16[32,2304]{1,0:T(8,128)(2,1)}) %reduce-scatter.8.cloned.1.call-update) | async-done | bytes 147472 | tf_op jit(solution)/shard_map/reduce_scatter | solution.py:218
  447.9 1.7 select_convert_fusion
  (152 shorter events, 30.6 us)
Async XLA Ops:
  6.5 314.0 %copy-start = (bf16[1,360,2304]{2,1,0:T(8,128)(2,1)S(1)}, bf16[1,360,2304]{2,1,0:T(8,128)(2,1)}, u32[]{:S(2)}) copy-start(bf16[1,360,2304]{2,1,0:T(8,128)(2,1)} %param.39) | copy-start | bytes 4976644
  6.5 116.0 %all-gather.3.cloned.1.call-start = ((), (), s32[]{:S(2)}) async-start(), calls=%async_computation.6 | async-start | bytes 4456448 | tf_op jit(solution)/shard_map/all_gather | solution.py:91
  9.5 3.5 copy-start.1
  11.9 0.7 copy-start.16
  12.7 10.4 %copy-start.27 = (u32[128]{0:T(128)S(1)}, u32[128]{0:T(128)}, u32[]{:S(2)}) copy-start(u32[128]{0:T(128)} %constant.214) | copy-start | bytes 1540
  12.7 11.7 %copy-start.24 = (s32[8]{0:T(128)S(1)}, s32[8]{0:T(128)}, u32[]{:S(2)}) copy-start(s32[8]{0:T(128)} %param.31) | copy-start | bytes 100
  12.7 29.3 %copy-start.2 = (s32[8]{0:T(128)S(1)}, s32[8]{0:T(128)}, u32[]{:S(2)}) copy-start(s32[8]{0:T(128)} %param.33) | copy-start | bytes 100
  12.7 29.3 %copy-start.23 = (s32[2]{0:T(128)S(1)}, s32[2]{0:T(128)}, u32[]{:S(2)}) copy-start(s32[2]{0:T(128)} %param.30) | copy-start | bytes 28
  14.0 33.2 %copy-start.6 = (bf16[256,2304]{1,0:T(8,128)(2,1)S(1)}, bf16[256,2304]{1,0:T(8,128)(2,1)}, u32[]{:S(2)}) copy-start(bf16[256,2304]{1,0:T(8,128)(2,1)} %param.20) | copy-start | bytes 3538948
  14.9 47.3 %all-to-all-start = ((bf16[16,2,32,256]{3,2,1,0:T(8,128)(2,1)}), bf16[16,2,32,256]{3,2,1,0:T(8,128)(2,1)}, u32[]{:S(2)}, u32[]{:S(2)}) async-start(bf16[16,2,32,256]{3,2,1,0:T(8,128)(2,1)} %pad_maximum_fusion.1), calls=%async_computation | async-start | bytes 1048576 | tf_op jit(solution)/shard_map/all_to_all | solution.py:146
  44.9 4.7 %copy-start.7 = (bf16[2,2,1024,256]{3,2,1,0:T(8,128)(2,1)S(1)}, bf16[2,2,1024,256]{3,2,1,0:T(8,128)(2,1)}, u32[]{:S(2)}) copy-start(bf16[2,2,1024,256]{3,2,1,0:T(8,128)(2,1)} %param.28) | copy-start | bytes 6291460
  49.7 2.1 copy-start.19
  49.7 3.9 copy-start.9
  53.8 4.2 copy-start.10
  53.8 6.4 %copy-start.18 = (bf16[8,32,4,64]{3,2,1,0:T(4,128)(2,1)S(1)}, bf16[8,32,4,64]{3,2,1,0:T(4,128)(2,1)}, u32[]{:S(2)}) copy-start(bf16[8,32,4,64]{3,2,1,0:T(4,128)(2,1)} %reshape.409) | copy-start | bytes 393220
  68.9 2.7 copy-start.14
  68.9 2.7 copy-start.15
  78.9 2.0 copy-start.13
  82.8 2.5 copy-start.8
  87.6 6.6 %copy-start.26 = (f32[2304]{0:T(1024)S(1)}, f32[2304]{0:T(1024)}, u32[]{:S(2)}) copy-start(f32[2304]{0:T(1024)} %param.21) | copy-start | bytes 27652
  87.6 25.6 %all-to-all-start.1 = ((f32[16,2,32,260]{3,2,1,0:T(8,128)}), f32[16,2,32,260]{3,2,1,0:T(8,128)S(1)}, u32[]{:S(2)}, u32[]{:S(2)}) async-start(f32[16,2,32,260]{3,2,1,0:T(8,128)} %pad_maximum_fusion), calls=%async_computation.1 | async-start | bytes 3145728 | tf_op jit(solution)/shard_map/all_to_all | solution.py:164
  92.7 104.0 %reduce-scatter.4.cloned.1.call-start = ((), (), s32[]{:S(2)}) async-start(), calls=%async_computation.7 | async-start | bytes 2654208 | tf_op jit(solution)/shard_map/reduce_scatter | solution.py:180
  131.1 4.2 copy-start.17
  153.6 8.2 %copy-start.12 = (f32[1,256,4,64]{1,3,2,0:T(8,128)S(1)}, f32[1,256,4,64]{1,3,2,0:T(8,128)}, u32[]{:S(2)}) copy-start(f32[1,256,4,64]{1,3,2,0:T(8,128)} %copy.288) | copy-start | bytes 786436
  161.7 1.3 copy-start.11
  163.0 34.8 %copy-start.22 = (f32[2304]{0:T(1024)S(1)}, f32[2304]{0:T(1024)}, u32[]{:S(2)}) copy-start(f32[2304]{0:T(1024)} %param.34) | copy-start | bytes 27652
  164.9 35.0 %copy-start.21 = (s32[256,2]{0,1:T(2,128)S(1)}, s32[256,2]{0,1:T(2,128)}, u32[]{:S(2)}) copy-start(s32[256,2]{0,1:T(2,128)} %param.36) | copy-start | bytes 6148
  164.9 57.4 %all-gather.5.cloned.1.call-start = ((), (), s32[]{:S(2)}) async-start(), calls=%async_computation.8 | async-start | bytes 1327104 | tf_op jit(solution)/shard_map/all_gather | solution.py:183
  199.6 213.6 %reduce-scatter.6.cloned.1.call-start = ((), (), s32[]{:S(2)}) async-start(), calls=%async_computation.9 | async-start | bytes 7520256 | tf_op jit(solution)/shard_map/reduce_scatter | solution.py:213
  224.6 91.8 %copy-start.25 = (bf16[1,2304,360]{1,2,0:T(8,128)(2,1)S(1)}, bf16[1,2304,360]{1,2,0:T(8,128)(2,1)}, u32[]{:S(2)}) copy-start(bf16[1,2304,360]{1,2,0:T(8,128)(2,1)} %param.37) | copy-start | bytes 4976644
  313.5 2.9 copy-start.3
  333.7 1.3 copy-start.4
  333.7 1.3 copy-start.20
  333.7 114.2 %reduce-scatter.8.cloned.1.call-start = ((), (), s32[]{:S(2)}) async-start(), calls=%async_computation.10 | async-start | bytes 1327104 | tf_op jit(solution)/shard_map/reduce_scatter | solution.py:218
  339.5 108.4 %copy-start.5 = (f32[32,2304]{1,0:T(8,128)S(1)}, f32[32,2304]{1,0:T(8,128)}, u32[]{:S(2)}) copy-start(f32[32,2304]{1,0:T(8,128)} %reduce-scatter.4.cloned.1.call-done) | copy-start | bytes 884740
Sparse Core Ops, SparseCore 0:
  9.6 57.6 all-gather.2
  165.0 31.5 reduce-scatter.3
  199.7 22.5 all-gather.4
  333.8 79.3 reduce-scatter.5
  416.5 31.2 reduce-scatter.7
